TPU v7x, 512 devices: a whole 4x4x16 slice. The times are simulated.
512 devices in a mesh: seq: 32 (over z, core), mp: 16 (over y, x).
Axes of the slice: x: 4, y: 4, z: 16, core: 2. Of those that a mesh axis runs over, the one named last changes fastest.
Arguments:
- continued_prompt_entries: bfloat16 [4096, 4096], P('seq', 'mp'), may hold values from -6 to 6
- padded_prompt_entries: bfloat16 [4096, 4096], P('seq', 'mp'), may hold values from -6 to 6
- prompt_live_extents: int32 [64], P('seq'), may hold values from 8 to 64, as said below
- preceding_entry_line: bfloat16 [4096], P('mp'), may hold values from -6 to 6
- carried_memory: float32 [64, 64, 64], P('mp'), may hold values from -24 to 24
- token_mixing_ratios: float32 [5, 4096], replicated, may hold values from 0.05 to 0.95
- acceptance_transform: bfloat16 [4096, 4096], P('seq', 'mp'), may hold values from -0.09375 to 0.09375
- lookup_transform: bfloat16 [4096, 4096], P('seq', 'mp'), may hold values from -0.09375 to 0.09375
- payload_transform: bfloat16 [4096, 4096], P('seq', 'mp'), may hold values from -0.09375 to 0.09375
- gating_transform: bfloat16 [4096, 4096], P('seq', 'mp'), may hold values from -0.09375 to 0.09375
- fading_baseline: float32 [4096], P('mp'), may hold values from -10 to -3.5
- fading_left_factor: bfloat16 [4096, 128], replicated, may hold values from -0.09375 to 0.09375
- fading_right_factor: bfloat16 [128, 4096], P(None, 'mp'), may hold values from -0.5 to 0.5
- present_reward: float32 [64, 64], P('mp'), may hold values from -3 to 3
- group_layer_scaling: float32 [4096], P('mp'), may hold values from 0.5 to 1.5
- group_layer_shift_term: float32 [4096], P('mp'), may hold values from -1.8 to 1.8
- final_transform: bfloat16 [4096, 4096], P('mp', 'seq'), may hold values from -0.09375 to 0.09375
Outputs:
- mixed: bfloat16 [32, 256, 4096], P('seq', 'mp')
- span_states: float32 [32, 64, 64, 64], P('seq', 'mp')
- request_states: float32 [64, 64, 64, 64], P('seq', 'mp')
Inputs may be any that keep to these rules, and one draw needn't show every extreme that they name: `prompt_live_extents`: some request has all 64 rows live.
All inputs are finite; a program needn't handle non-finite values.
Results may differ from a plain program's by a relative error of at most 0.0076.
Values may be sent and summed in bfloat16 or wider, within the bound.
A program may use at most 64 MiB of HBM per device.

v0:
```python
import jax
import jax.numpy as jnp
from jax import lax
from jax.sharding import PartitionSpec as P

BLK = 64
norm_eps = 0.00064
highest = lax.Precision.HIGHEST


def passed_along(x, axis, by):
    length = lax.axis_size(axis)
    pairs = [(i, i + by) for i in range(length) if 0 <= i + by < length]
    return lax.ppermute(x, axis, pairs)


def entering(value, axis, join, neutral):
    count, mine = (lax.axis_size(axis), lax.axis_index(axis))
    pieces = jax.tree.map(lambda part: lax.all_gather(part, axis), value)
    total = jax.tree.map(
        lambda part, zero: jnp.full_like(part, 0) + jnp.asarray(zero, part.dtype), value, neutral
    )

    def hop(position, total):
        longer = join(total, jax.tree.map(lambda part: part[position], pieces))
        return jax.tree.map(lambda new, old: jnp.where(position < mine, new, old), longer, total)

    return lax.fori_loop(0, count - 1, hop, total)


def mix_rows(current, previous, weight):
    here = current.astype(jnp.float32)
    return (here + weight[None, :] * (previous.astype(jnp.float32) - here)).astype(jnp.bfloat16)


def block_sweep(
    evolving_memory,
    acceptance_entries,
    lookup_entries,
    payload_entries,
    log_fading_amount,
    diagonal_reward,
):
    inclusive = jnp.cumsum(log_fading_amount, axis=0)
    exclusive = inclusive - log_fading_amount
    recept_scaled = acceptance_entries * jnp.exp(exclusive)
    keys_scaled = lookup_entries * jnp.exp(-inclusive)
    scores = jnp.einsum("ihc,jhc->hij", recept_scaled, keys_scaled, precision=highest)
    count = acceptance_entries.shape[0]
    row_index = lax.broadcasted_iota(jnp.int32, (count, count), 0)
    col_index = lax.broadcasted_iota(jnp.int32, (count, count), 1)
    scores = jnp.where((row_index > col_index)[None], scores, 0.0)
    diagonal_contribution = jnp.sum(
        acceptance_entries * diagonal_reward[None] * lookup_entries, axis=-1, keepdims=True
    )
    answer_lines = (
        jnp.einsum("hij,jhd->ihd", scores, payload_entries, precision=highest)
        + diagonal_contribution * payload_entries
    )
    answer_lines = answer_lines + jnp.einsum(
        "ihc,hcd->ihd", recept_scaled, evolving_memory, precision=highest
    )
    total = inclusive[-1]
    carried = lookup_entries * jnp.exp(total[None] - inclusive)
    new_state = jnp.exp(total)[:, :, None] * evolving_memory + jnp.einsum(
        "jhc,jhd->hcd", carried, payload_entries, precision=highest
    )
    return (new_state, answer_lines)


def continued_recurrence(
    acceptance_entries, lookup_entries, payload_entries, log_fading_amount, diagonal_reward
):
    length, per_group_view, embedding_dimension = acceptance_entries.shape
    blocks = length // BLK

    def step(evolving_memory, entry_lines):
        return block_sweep(
            evolving_memory,
            entry_lines[0],
            entry_lines[1],
            entry_lines[2],
            entry_lines[3],
            diagonal_reward,
        )

    shaped = tuple(
        (
            a.reshape(blocks, BLK, per_group_view, embedding_dimension)
            for a in (acceptance_entries, lookup_entries, payload_entries, log_fading_amount)
        )
    )
    evolving_memory, results = lax.scan(
        step,
        jnp.zeros((per_group_view, embedding_dimension, embedding_dimension), jnp.float32),
        shaped,
    )
    return (evolving_memory, results.reshape(length, per_group_view, embedding_dimension))


def combine(earlier, later):
    return (earlier[0] + later[0], jnp.exp(later[0])[:, :, None] * earlier[1] + later[1])


def shifted_rows(current, edge_row, long_rows, requests, slot_rows):
    feature_part = current.shape[1]
    long_prev = jnp.concatenate([edge_row, current[: long_rows - 1]], axis=0)
    short_view = current[long_rows:].reshape(requests, slot_rows, feature_part)
    short_prev = jnp.concatenate(
        [jnp.zeros((requests, 1, feature_part), current.dtype), short_view[:, :-1]], axis=1
    )
    short_prev = short_prev.reshape(requests * slot_rows, feature_part)
    return jnp.concatenate([long_prev, short_prev], axis=0)


def on_device(
    continued_prompt_entries,
    padded_prompt_entries,
    prompt_live_extents,
    preceding_entry_line,
    carried_memory,
    token_mixing_ratios,
    acceptance_transform,
    lookup_transform,
    payload_transform,
    gating_transform,
    fading_baseline,
    fading_left_factor,
    fading_right_factor,
    present_reward,
    group_layer_scaling,
    group_layer_shift_term,
    final_transform,
):
    long_rows = continued_prompt_entries.shape[0]
    requests = prompt_live_extents.shape[0]
    slot_rows = padded_prompt_entries.shape[0] // requests
    per_group_view, embedding_dimension = present_reward.shape
    arrived = passed_along(continued_prompt_entries[-1:], "seq", 1)
    first = lax.axis_index("seq") == 0
    edge_row = jnp.where(first, preceding_entry_line[None, :], arrived)
    current = jnp.concatenate([continued_prompt_entries, padded_prompt_entries], axis=0)
    current, edge_full = (
        lax.all_gather(current, "mp", axis=1, tiled=True),
        lax.all_gather(edge_row, "mp", axis=1, tiled=True),
    )
    previous = shifted_rows(current, edge_full, long_rows, requests, slot_rows)
    mixes = [mix_rows(current, previous, token_mixing_ratios[index]) for index in range(5)]
    total_rows = current.shape[0]
    columns = acceptance_transform.shape[1]
    pieces = (
        lax.all_gather(acceptance_transform, "seq", axis=0, tiled=True),
        lax.all_gather(lookup_transform, "seq", axis=0, tiled=True),
        lax.all_gather(payload_transform, "seq", axis=0, tiled=True),
        lax.all_gather(gating_transform, "seq", axis=0, tiled=True),
    )
    acceptance_entries, lookup_entries, payload_entries, gate = tuple(
        (
            jnp.dot(source, piece, preferred_element_type=jnp.float32)
            for source, piece in zip(mixes[:4], pieces)
        )
    )
    squeezed = jnp.tanh(
        jnp.dot(mixes[4], fading_left_factor, preferred_element_type=jnp.float32)
    ).astype(jnp.bfloat16)
    log_fading_amount = -jnp.exp(
        fading_baseline[None, :]
        + jnp.dot(squeezed, fading_right_factor, preferred_element_type=jnp.float32)
    )
    recept3, keys3, values3, decay3 = [
        a.reshape(total_rows, per_group_view, embedding_dimension)
        for a in (acceptance_entries, lookup_entries, payload_entries, log_fading_amount)
    ]
    local_state, long_out = continued_recurrence(
        recept3[:long_rows],
        keys3[:long_rows],
        values3[:long_rows],
        decay3[:long_rows],
        present_reward,
    )
    long_decay = decay3[:long_rows]
    group_total = jnp.sum(long_decay, axis=0)
    blank = (
        jnp.zeros((per_group_view, embedding_dimension), jnp.float32),
        jnp.zeros((per_group_view, embedding_dimension, embedding_dimension), jnp.float32),
    )
    prefix_total, prefix_state = entering((group_total, local_state), "seq", combine, blank)
    incoming = jnp.exp(prefix_total)[:, :, None] * carried_memory + prefix_state
    before_row = jnp.cumsum(long_decay, axis=0) - long_decay
    long_out = long_out + jnp.einsum(
        "ihc,hcd->ihd", recept3[:long_rows] * jnp.exp(before_row), incoming, precision=highest
    )
    span_end = jnp.exp(group_total)[:, :, None] * incoming + local_state
    live_rows = (
        lax.broadcasted_iota(jnp.int32, (requests, slot_rows), 1) < prompt_live_extents[:, None]
    )
    live_flat = live_rows.reshape(requests * slot_rows).astype(jnp.float32)[:, None, None]
    short_shape = (requests, slot_rows, per_group_view, embedding_dimension)
    short_recept = recept3[long_rows:].reshape(short_shape)
    short_keys = (keys3[long_rows:] * live_flat).reshape(short_shape)
    short_values = values3[long_rows:].reshape(short_shape)
    short_decay = (decay3[long_rows:] * live_flat).reshape(short_shape)
    zeroed_memory = jnp.zeros(
        (per_group_view, embedding_dimension, embedding_dimension), jnp.float32
    )

    def request_pass(acceptance_lines, lookup_table, payload_table, fading_table):
        return block_sweep(
            zeroed_memory,
            acceptance_lines,
            lookup_table,
            payload_table,
            fading_table,
            present_reward,
        )

    request_states, short_out = jax.vmap(request_pass)(
        short_recept, short_keys, short_values, short_decay
    )
    wkv = jnp.concatenate(
        [long_out, short_out.reshape(requests * slot_rows, per_group_view, embedding_dimension)],
        axis=0,
    )
    mean = jnp.mean(wkv, axis=-1, keepdims=True)
    centred = wkv - mean
    variance = jnp.mean(centred * centred, axis=-1, keepdims=True)
    normed = (centred * lax.rsqrt(variance + norm_eps)).reshape(
        total_rows, columns
    ) * group_layer_scaling[None, :] + group_layer_shift_term[None, :]
    row_live = jnp.concatenate(
        [jnp.ones((long_rows,), dtype=bool), live_rows.reshape(requests * slot_rows)], axis=0
    )
    hidden = jnp.where(row_live[:, None], normed * jax.nn.silu(gate), 0.0).astype(jnp.bfloat16)
    full_out = lax.all_gather(final_transform, "seq", axis=1, tiled=True)
    mixed_rows = lax.psum_scatter(
        jnp.dot(hidden, full_out, preferred_element_type=jnp.float32),
        "mp",
        scatter_dimension=0,
        tiled=True,
    )
    return (mixed_rows.astype(jnp.bfloat16)[None], span_end[None], request_states)


def solution(mesh):
    placed = (
        P("seq", "mp"),
        P("seq", "mp"),
        P("seq"),
        P("mp"),
        P("mp", None, None),
        P(),
        P("seq", "mp"),
        P("seq", "mp"),
        P("seq", "mp"),
        P("seq", "mp"),
        P("mp"),
        P(),
        P(None, "mp"),
        P("mp", None),
        P("mp"),
        P("mp"),
        P("mp", "seq"),
    )
    return jax.shard_map(
        on_device,
        mesh=mesh,
        in_specs=placed,
        out_specs=(P("seq", "mp", None), P("seq", "mp", None, None), P("seq", "mp", None, None)),
        check_vma=False,
    )
```

profile of v0, /device:TPU:2, one launch (start us, length us, event | category | flops | bytes accessed | tf_op | source)
XLA Modules:
  0.0 631.1 jit_solution(9215683122175775181)
XLA Ops:
  7.2 1.6 pad_maximum_fusion.2
  11.7 1.7 collective-permute-start
  13.4 1.9 fusion.85
  16.0 27.3 %all_gather.34 = bf16[1,4096]{1,0:T(2,128)(2,1)} all-gather(bf16[1,256]{1,0:T(2,128)(2,1)S(1)} %broadcast_select_fusion), channel_id=1, replica_groups=mesh['seq'=32,'mp'=16] {'mp'}, dimensions={1}, use_global_device_ids=true | all-gather | bytes 8704 | tf_op jit(solution)/shard_map/all_gather | solution.py:145
  43.3 35.5 %all-gather.9.cloned.1.call-done = bf16[256,4096]{1,0:T(8,128)(2,1)} async-done(((bf16[256,256]{1,0:T(8,128)(2,1)}), bf16[256,4096]{1,0:T(8,128)(2,1)}) %all-gather.9.cloned.1.call-update) | async-done | bytes 2097168 | tf_op jit(solution)/shard_map/all_gather | solution.py:144
  78.7 1.5 slice.100
  80.2 1.2 concatenate.24
  82.5 3.0 fusion.41
  85.5 1.3 slice_reduce_fusion
  87.9 64.6 %all-gather.15.cloned.1.call-done = bf16[4096,256]{1,0:T(8,128)(2,1)} async-done(((bf16[128,256]{1,0:T(8,128)(2,1)}), bf16[4096,256]{1,0:T(8,128)(2,1)}) %all-gather.15.cloned.1.call-update) | async-done | bytes 2097168 | tf_op jit(solution)/shard_map/all_gather | solution.py:152
  152.5 3.7 fusion.25
  157.0 66.3 %all-gather.11.cloned.1.call-done = bf16[4096,256]{1,0:T(8,128)(2,1)} async-done(((bf16[128,256]{1,0:T(8,128)(2,1)}), bf16[4096,256]{1,0:T(8,128)(2,1)}) %all-gather.11.cloned.1.call-update) | async-done | bytes 2097168 | tf_op jit(solution)/shard_map/all_gather | solution.py:153
  223.3 4.0 fusion.29
  228.2 65.8 %all-gather.13.cloned.1.call-done = bf16[4096,256]{1,0:T(8,128)(2,1)} async-done(((bf16[128,256]{1,0:T(8,128)(2,1)}), bf16[4096,256]{1,0:T(8,128)(2,1)}) %all-gather.13.cloned.1.call-update) | async-done | bytes 2097168 | tf_op jit(solution)/shard_map/all_gather | solution.py:154
  294.0 3.6 fusion.27
  298.5 13.3 %while.29 = (s32[]{:T(128)}, f32[4,64,64]{2,1,0:T(8,128)S(1)}, f32[2,64,4,64]{1,0,3,2:T(2,128)}, f32[2,64,4,64]{1,0,3,2:T(2,128)S(1)}, f32[2,64,4,64]{3,2,1,0:T(...) while((s32[]{:T(128)}, f32[4,64,64]{2,1,0:T(8,128)S(1)}, ...), condition=%wide.region_3.4_spmd.clone, body=%wide.region_0.3_spmd.clone.sunk | while | flops 51646208 | bytes 2444416 | solution.py:93
  300.4 4.3 dynamic_update_slice.6
  307.1 4.3 dynamic_update_slice.6
  314.7 32.2 %all_gather.39 = f32[32,4,64]{2,1,0:T(4,128)} all-gather(f32[1,4,64]{2,1,0:T(4,128)S(1)} %all_gather.38), channel_id=1, replica_groups=mesh['seq'=32,'mp'=16] {'seq'}, dimensions={0}, use_global_device_ids=true | all-gather | bytes 33792 | tf_op jit(solution)/shard_map/all_gather | solution.py:19
  347.6 1.2 reshape.144
  358.3 25.6 %all-gather.21.cloned.1.call-done = f32[128,64,64]{2,1,0:T(8,128)} async-done(((f32[4,64,64]{2,1,0:T(8,128)}), f32[128,64,64]{2,1,0:T(8,128)}) %all-gather.21.cloned.1.call-update) | async-done | bytes 2097168 | tf_op jit(solution)/shard_map/all_gather | solution.py:19
  383.9 53.9 %while.30 = (s32[]{:T(128)}, f32[4,64]{1,0:T(4,128)S(1)}, f32[4,64,64]{2,1,0:T(8,128)S(1)}, s32[]{:T(128)}, f32[32,4,64]{2,1,0:T(4,128)}, /*index=5*/f32[32,4,64,64]{3,2,1,0:T(8,128)}, s32[]{:T(128)}, s32[]{:T(128)}) while((s32[]{:T(128)}, f32[4,64]{1,0:T(4,128)S(1)}, f32[4,64,64]{2,1,0:T(8,128)S(1)}, s32[]{:T(128)}, ...), condition=%wide.region_6.7_spmd.clone, body=%wide.region_5.6_spmd.clone.sunk | while | flops 66308 | bytes 201843 | solution.py:28
  437.8 1.8 fusion.42
  442.3 1.8 copy.102
  444.8 1.8 copy.101
  446.5 1.7 copy.99
  448.2 5.8 all-gather.17.cloned.1.call-done
  454.0 72.6 %all-gather.19.cloned.1.call-done = bf16[256,4096]{1,0:T(8,128)(2,1)} async-done(((bf16[256,128]{1,0:T(8,128)(2,1)}), bf16[256,4096]{1,0:T(8,128)(2,1)}) %all-gather.19.cloned.1.call-update) | async-done | bytes 2097168 | tf_op jit(solution)/shard_map/all_gather | solution.py:234
  526.5 7.5 %fusion.63 = f32[256,4096]{1,0:T(8,128)} fusion(bf16[256,4096]{1,0:T(8,128)(2,1)} %all-gather.19.cloned.1.call-done, f32[256,256]{1,0:T(8,128)} %copy.102, f32[256,256]{1,0:T(8,128)} %copy.101, f32[128,256]{1,0:T(8,128)} %concatenate.27, f32[128,256]{1,0:T(8,128)} %copy.99, bf16[4096,256]{1,0:T(8,128)(2,1)} %all-gather.17.cloned.1.call-done, ...), kind=kOutput, calls=%fused_computation.83 | convolution fusion | flops 1086062592 | bytes 13388032 | tf_op jit(solution)/shard_map/dot_general | solution.py:236
  535.0 1.3 convolution_add_fusion.1
  537.1 85.6 %reduce-scatter.2.cloned.1.call-done = f32[16,4096]{1,0:T(8,128)} async-done(((f32[256,4096]{1,0:T(8,128)}), f32[16,4096]{1,0:T(8,128)}) %reduce-scatter.2.cloned.1.call-update) | async-done | bytes 262160 | tf_op jit(solution)/shard_map/reduce_scatter | solution.py:235
  622.7 1.6 convert_bitcast_fusion
  (196 shorter events, 83.7 us)
Async XLA Ops:
  7.2 75.3 %copy-start = (bf16[4096,128]{1,0:T(8,128)(2,1)S(1)}, bf16[4096,128]{1,0:T(8,128)(2,1)}, u32[]{:S(2)}) copy-start(bf16[4096,128]{1,0:T(8,128)(2,1)} %param.32) | copy-start | bytes 3145732
  7.2 71.5 %all-gather.9.cloned.1.call-start = ((), (), s32[]{:S(2)}) async-start(), calls=%async_computation.1 | async-start | bytes 2228224 | tf_op jit(solution)/shard_map/all_gather | solution.py:144
  8.9 143.6 %all-gather.15.cloned.1.call-start = ((), (), s32[]{:S(2)}) async-start(), calls=%async_computation.4 | async-start | bytes 2162688 | tf_op jit(solution)/shard_map/all_gather | solution.py:152
  9.6 213.7 %all-gather.11.cloned.1.call-start = ((), (), s32[]{:S(2)}) async-start(), calls=%async_computation.2 | async-start | bytes 2162688 | tf_op jit(solution)/shard_map/all_gather | solution.py:153
  10.4 283.7 %all-gather.13.cloned.1.call-start = ((), (), s32[]{:S(2)}) async-start(), calls=%async_computation.3 | async-start | bytes 2162688 | tf_op jit(solution)/shard_map/all_gather | solution.py:154
  10.9 372.9 %all-gather.21.cloned.1.call-start = ((), (), s32[]{:S(2)}) async-start(), calls=%async_computation.8 | async-start | bytes 4325376 | tf_op jit(solution)/shard_map/all_gather | solution.py:19
  11.7 3.7 collective-permute-start
  78.7 2.7 copy-start.3
  223.3 70.7 %copy-start.8 = (bf16[2,64,4096]{2,1,0:T(8,128)(2,1)S(1)}, bf16[2,64,4096]{2,1,0:T(8,128)(2,1)}, u32[]{:S(2)}) copy-start(bf16[2,64,4096]{2,1,0:T(8,128)(2,1)} %concatenate.24) | copy-start | bytes 3145732
  223.3 70.7 %copy-start.14 = (bf16[1,4096]{1,0:T(2,128)(2,1)S(1)}, bf16[1,4096]{1,0:T(2,128)(2,1)}, u32[]{:S(2)}) copy-start(bf16[1,4096]{1,0:T(2,128)(2,1)} %all_gather.34) | copy-start | bytes 24580
  294.0 4.5 copy-start.13
  298.5 15.4 %copy-start.16 = (s32[2]{0:T(128)S(1)}, s32[2]{0:T(128)}, u32[]{:S(2)}) copy-start(s32[2]{0:T(128)} %param.23) | copy-start | bytes 28
  298.5 16.1 %copy-start.15 = (f32[256]{0:T(256)S(1)}, f32[256]{0:T(256)}, u32[]{:S(2)}) copy-start(f32[256]{0:T(256)} %get-tuple-element.272) | copy-start | bytes 3076
  298.5 48.3 %copy-start.6 = (f32[128,256]{0,1:T(8,128)S(1)}, f32[128,256]{0,1:T(8,128)}, u32[]{:S(2)}) copy-start(f32[128,256]{0,1:T(8,128)} %get-tuple-element.274) | copy-start | bytes 393220
  298.5 48.5 %copy-start.10 = (f32[128,256]{0,1:T(8,128)S(1)}, f32[128,256]{0,1:T(8,128)}, u32[]{:S(2)}) copy-start(f32[128,256]{0,1:T(8,128)} %get-tuple-element.273) | copy-start | bytes 393220
  311.8 0.7 copy-start.1
  312.5 141.5 %all-gather.17.cloned.1.call-start = ((), (), s32[]{:S(2)}) async-start(), calls=%async_computation.5 | async-start | bytes 2162688 | tf_op jit(solution)/shard_map/all_gather | solution.py:155
  313.0 213.5 %all-gather.19.cloned.1.call-start = ((), (), s32[]{:S(2)}) async-start(), calls=%async_computation.6 | async-start | bytes 2162688 | tf_op jit(solution)/shard_map/all_gather | solution.py:234
  313.8 308.9 %reduce-scatter.2.cloned.1.call-start = ((), (), s32[]{:S(2)}) async-start(), calls=%async_computation.7 | async-start | bytes 4456448 | tf_op jit(solution)/shard_map/reduce_scatter | solution.py:235
  347.3 7.4 %copy-start.12 = (f32[2,64,4,64]{1,0,3,2:T(2,128)S(1)}, f32[2,64,4,64]{1,0,3,2:T(2,128)}, u32[]{:S(2)}) copy-start(f32[2,64,4,64]{1,0,3,2:T(2,128)} %get-tuple-element.156) | copy-start | bytes 393220
  347.5 5.4 copy-start.7
  354.6 171.9 %copy-start.17 = (f32[256]{0:T(256)S(1)}, f32[256]{0:T(256)}, u32[]{:S(2)}) copy-start(f32[256]{0:T(256)} %param.36) | copy-start | bytes 3076
  358.3 168.2 %copy-start.4 = (bf16[256,4096]{1,0:T(8,128)(2,1)S(1)}, bf16[256,4096]{1,0:T(8,128)(2,1)}, u32[]{:S(2)}) copy-start(bf16[256,4096]{1,0:T(8,128)(2,1)} %all-gather.9.cloned.1.call-done) | copy-start | bytes 6291460
  439.6 1.0 copy-start.5
  534.0 0.9 copy-start.9
  534.0 2.3 copy-start.2
  534.0 2.3 copy-start.11
Sparse Core Ops, SparseCore 0:
  11.6 67.0 all-gather.8
  80.8 71.5 all-gather.14
  154.6 68.6 all-gather.10
  225.3 68.6 all-gather.12
  312.6 71.2 all-gather.20
  385.8 68.0 all-gather.16
  456.0 70.4 all-gather.18
  534.2 88.4 reduce-scatter.1
where the time goes:
time: 633 us; the launch traced here: 631 us
  waiting for transfers between devices  425 us (67%)
  other arithmetic  64.5 us (10%)
  blocking collectives  59.4 us (9%)
  local copies, waits for them, and re-layouts  35.3 us (6%)
  matrix products  29.4 us (5%)
  between operations  14.5 us (2%)
    reduce_scatter x1, waiting for transfers between devices, on_device(): lax.psum_scatter(jnp.dot(hidden, full_out, preferred_element_type=jnp.flo...  85.6 us
    all_gather x1, waiting for transfers between devices, on_device(): full_out = lax.all_gather(final_transform, 'seq', axis=1, tiled=True)  72.6 us
    all_gather x1, waiting for transfers between devices, on_device(): lax.all_gather(lookup_transform, 'seq', axis=0, tiled=True)  66.3 us
    all_gather x1, waiting for transfers between devices, on_device(): lax.all_gather(payload_transform, 'seq', axis=0, tiled=True)  65.8 us
    all_gather x1, waiting for transfers between devices, on_device(): lax.all_gather(acceptance_transform, 'seq', axis=0, tiled=True)  64.6 us
    all_gather x1, waiting for transfers between devices, on_device(): lax.all_gather(current, 'mp', axis=1, tiled=True)  35.5 us
    all_gather x1, blocking collectives, entering(): pieces = jax.tree.map(lambda part: lax.all_gather(part, axis), value)  32.2 us
    select_n x31, other arithmetic, hop(): jnp.where(position < mine, new, old)  32 us
  transfers between devices with their start and end apart: 9, of which 8 were waited for; matrix products, arithmetic and copies ran while one was open for 16% of the time, Pallas kernels for 0%

commit v1 on v0

--- a/solution.py
+++ b/solution.py
@@ -6,6 +6,12 @@
 BLK = 64
 norm_eps = 0.00064
 highest = lax.Precision.HIGHEST
+
+
+def detail_lines(frame):
+    built = jnp.concatenate([frame for _ in range(lax.axis_size("mp"))], 1)
+    left_arr = lax.all_to_all(built, "mp", 1, 1, tiled=True)
+    return left_arr
 
 
 def passed_along(x, axis, by):
@@ -140,10 +146,7 @@
     first = lax.axis_index("seq") == 0
     edge_row = jnp.where(first, preceding_entry_line[None, :], arrived)
     current = jnp.concatenate([continued_prompt_entries, padded_prompt_entries], axis=0)
-    current, edge_full = (
-        lax.all_gather(current, "mp", axis=1, tiled=True),
-        lax.all_gather(edge_row, "mp", axis=1, tiled=True),
-    )
+    current, edge_full = (detail_lines(current), lax.all_gather(edge_row, "mp", axis=1, tiled=True))
     previous = shifted_rows(current, edge_full, long_rows, requests, slot_rows)
     mixes = [mix_rows(current, previous, token_mixing_ratios[index]) for index in range(5)]
     total_rows = current.shape[0]

time: 633 us -> 573 us (0.905)
  waiting for transfers between devices: 425 us -> 324 us
  local copies, waits for them, and re-layouts: 35.3 us -> 48.9 us
  blocking collectives: 59.4 us -> 71.9 us
  starting transfers between devices: 2.04 us -> 11.1 us
  matrix products: 29.4 us -> 35.8 us
    all_gather x1, waiting for transfers between devices: 64.6 us -> 0.02 us  [on_device(): lax.all_gather(acceptance_transform, 'seq', axis=0, tiled=True)]
    all_gather x1 -> x0, waiting for transfers between devices: 35.5 us -> none  [on_device(): lax.all_gather(current, 'mp', axis=1, tiled=True)]
    all_gather x1, blocking collectives: 27.3 us -> 40.2 us  [on_device(): lax.all_gather(edge_row, 'mp', axis=1, tiled=True)]
    all_to_all x0 -> x1, starting transfers between devices: none -> 9.55 us  [detail_lines(): left_arr = lax.all_to_all(built, 'mp', 1, 1, tiled=True)]
  transfers between devices with their start and end apart: 9 -> 9, of which waited for: 8 -> 7; matrix products, arithmetic and copies ran while one was open for 16% -> 20% of each run, Pallas kernels for 0% -> 0%
where the time goes in v1:
time: 573 us; the launch traced here: 570 us
  waiting for transfers between devices  324 us (57%)
  blocking collectives  71.9 us (13%)
  other arithmetic  62.9 us (11%)
  local copies, waits for them, and re-layouts  48.9 us (9%)
  matrix products  35.8 us (6%)
  between operations  14.7 us (3%)
  starting transfers between devices  11.1 us (2%)
    reduce_scatter x1, waiting for transfers between devices, on_device(): lax.psum_scatter(jnp.dot(hidden, full_out, preferred_element_type=jnp.flo...  85.1 us
    all_gather x1, waiting for transfers between devices, on_device(): full_out = lax.all_gather(final_transform, 'seq', axis=1, tiled=True)  72.5 us
    all_gather x1, waiting for transfers between devices, on_device(): lax.all_gather(payload_transform, 'seq', axis=0, tiled=True)  65.3 us
    all_gather x1, waiting for transfers between devices, on_device(): lax.all_gather(lookup_transform, 'seq', axis=0, tiled=True)  64.3 us
    all_gather x1, blocking collectives, on_device(): lax.all_gather(edge_row, 'mp', axis=1, tiled=True)  40.2 us
    select_n x31, other arithmetic, hop(): jnp.where(position < mine, new, old)  32 us
    all_gather x1, blocking collectives, entering(): pieces = jax.tree.map(lambda part: lax.all_gather(part, axis), value)  31.8 us
    all_gather x1, waiting for transfers between devices, entering(): pieces = jax.tree.map(lambda part: lax.all_gather(part, axis), value)  26.7 us
  transfers between devices with their start and end apart: 9, of which 7 were waited for; matrix products, arithmetic and copies ran while one was open for 20% of the time, Pallas kernels for 0%

profile of v1, /device:TPU:2, one launch (start us, length us, event | category | flops | bytes accessed | tf_op | source)
XLA Modules:
  0.0 570.2 jit_solution(7174210874886913070)
XLA Ops:
  11.0 2.4 copy.154
  13.4 9.5 %all-to-all-start = ((bf16[256,16,256]{2,0,1:T(8,128)(2,1)}), bf16[256,16,256]{2,0,1:T(8,128)(2,1)S(1)}, u32[]{:S(2)}, u32[]{:S(2)}) async-start(bf16[256,16,256]{2,0,1:T(8,128)(2,1)} %copy.154), calls=%async_computation | async-start | bytes 4194304 | tf_op jit(solution)/shard_map/all_to_all | solution.py:13
  26.9 40.2 %all_gather.30 = bf16[1,4096]{0,1:T(8,128)(2,1)} all-gather(bf16[1,256]{0,1:T(8,128)(2,1)S(1)} %reshape_select_fusion), channel_id=1, replica_groups=mesh['seq'=32,'mp'=16] {'mp'}, dimensions={1}, use_global_device_ids=true | all-gather | bytes 8704 | tf_op jit(solution)/shard_map/all_gather | solution.py:149
  67.1 1.6 copy.159
  68.7 2.3 reshape.143
  71.0 2.5 concatenate.28
  73.5 2.3 copy.160
  75.8 2.4 copy.155
  78.2 2.5 slice.104
  80.7 4.3 fusion.41
  87.4 5.0 fusion.25
  93.1 64.3 %all-gather.8.cloned.1.call-done = bf16[4096,256]{1,0:T(8,128)(2,1)} async-done(((bf16[128,256]{1,0:T(8,128)(2,1)}), bf16[4096,256]{1,0:T(8,128)(2,1)}) %all-gather.8.cloned.1.call-update) | async-done | bytes 2097168 | tf_op jit(solution)/shard_map/all_gather | solution.py:156
  157.4 4.8 fusion.29
  162.9 65.3 %all-gather.10.cloned.1.call-done = bf16[4096,256]{1,0:T(8,128)(2,1)} async-done(((bf16[128,256]{1,0:T(8,128)(2,1)}), bf16[4096,256]{1,0:T(8,128)(2,1)}) %all-gather.10.cloned.1.call-update) | async-done | bytes 2097168 | tf_op jit(solution)/shard_map/all_gather | solution.py:157
  228.3 4.8 fusion.27
  235.4 13.5 %while.29 = (s32[]{:T(128)}, f32[4,64,64]{2,1,0:T(8,128)S(1)}, f32[2,64,4,64]{1,0,3,2:T(2,128)}, f32[2,64,4,64]{1,0,3,2:T(2,128)S(1)}, f32[2,64,4,64]{3,2,1,0:T(...) while((s32[]{:T(128)}, f32[4,64,64]{2,1,0:T(8,128)S(1)}, ...), condition=%wide.region_3.4_spmd.clone, body=%wide.region_0.3_spmd.clone.sunk | while | flops 51646208 | bytes 2444416 | solution.py:99
  237.6 4.3 dynamic_update_slice.6
  244.2 4.3 dynamic_update_slice.6
  253.6 31.8 %all_gather.35 = f32[32,4,64]{2,1,0:T(4,128)} all-gather(f32[1,4,64]{2,1,0:T(4,128)S(1)} %all_gather.34), channel_id=1, replica_groups=mesh['seq'=32,'mp'=16] {'seq'}, dimensions={0}, use_global_device_ids=true | all-gather | bytes 33792 | tf_op jit(solution)/shard_map/all_gather | solution.py:25
  286.4 1.7 exponential_multiply_fusion
  294.1 26.7 %all-gather.18.cloned.1.call-done = f32[128,64,64]{2,1,0:T(8,128)} async-done(((f32[4,64,64]{2,1,0:T(8,128)}), f32[128,64,64]{2,1,0:T(8,128)}) %all-gather.18.cloned.1.call-update) | async-done | bytes 2097168 | tf_op jit(solution)/shard_map/all_gather | solution.py:25
  320.8 53.6 %while.30 = (s32[]{:T(128)}, f32[4,64]{1,0:T(4,128)S(1)}, f32[4,64,64]{2,1,0:T(8,128)S(1)}, s32[]{:T(128)}, f32[32,4,64]{2,1,0:T(4,128)}, /*index=5*/f32[32,4,64,64]{3,2,1,0:T(8,128)}, s32[]{:T(128)}, s32[]{:T(128)}) while((s32[]{:T(128)}, f32[4,64]{1,0:T(4,128)S(1)}, f32[4,64,64]{2,1,0:T(8,128)S(1)}, s32[]{:T(128)}, ...), condition=%wide.region_6.7_spmd.clone, body=%wide.region_5.6_spmd.clone.sunk | while | flops 66308 | bytes 201843 | solution.py:34
  374.5 1.9 fusion.42
  379.1 1.8 copy.183
  381.6 1.8 copy.182
  383.5 1.7 copy.180
  385.1 6.2 %all-gather.14.cloned.1.call-done = bf16[4096,256]{1,0:T(8,128)(2,1)} async-done(((bf16[128,256]{1,0:T(8,128)(2,1)}), bf16[4096,256]{1,0:T(8,128)(2,1)}) %all-gather.14.cloned.1.call-update) | async-done | bytes 2097168 | tf_op jit(solution)/shard_map/all_gather | solution.py:158
  391.3 72.5 %all-gather.16.cloned.1.call-done = bf16[256,4096]{1,0:T(8,128)(2,1)} async-done(((bf16[256,128]{1,0:T(8,128)(2,1)}), bf16[256,4096]{1,0:T(8,128)(2,1)}) %all-gather.16.cloned.1.call-update) | async-done | bytes 2097168 | tf_op jit(solution)/shard_map/all_gather | solution.py:237
  463.8 9.2 %fusion.63 = f32[256,4096]{1,0:T(8,128)} fusion(bf16[256,4096]{1,0:T(8,128)(2,1)} %all-gather.16.cloned.1.call-done, f32[256,256]{1,0:T(8,128)} %copy.183, f32[256,256]{1,0:T(8,128)} %copy.182, f32[128,256]{1,0:T(8,128)} %concatenate.31, f32[128,256]{1,0:T(8,128)} %copy.180, bf16[4096,256]{1,0:T(8,128)(2,1)} %all-gather.14.cloned.1.call-done, ...), kind=kOutput, calls=%fused_computation.83 | convolution fusion | flops 1086062592 | bytes 13388032 | tf_op jit(solution)/shard_map/dot_general | solution.py:239
  474.5 1.3 convolution_add_fusion.1
  476.6 85.1 %reduce-scatter.2.cloned.1.call-done = f32[16,4096]{1,0:T(8,128)} async-done(((f32[256,4096]{1,0:T(8,128)}), f32[16,4096]{1,0:T(8,128)}) %reduce-scatter.2.cloned.1.call-update) | async-done | bytes 262160 | tf_op jit(solution)/shard_map/reduce_scatter | solution.py:238
  561.7 1.6 convert_bitcast_fusion
  (228 shorter events, 88.0 us)
Async XLA Ops:
  7.2 73.5 %copy-start = (bf16[4096,128]{1,0:T(8,128)(2,1)S(1)}, bf16[4096,128]{1,0:T(8,128)(2,1)}, u32[]{:S(2)}) copy-start(bf16[4096,128]{1,0:T(8,128)(2,1)} %param.32) | copy-start | bytes 3145732
  7.2 80.2 %all-gather.12.cloned.1.call-start = ((), (), s32[]{:S(2)}) async-start(), calls=%async_computation.4 | async-start | bytes 2162688 | tf_op jit(solution)/shard_map/all_gather | solution.py:155
  7.9 149.5 %all-gather.8.cloned.1.call-start = ((), (), s32[]{:S(2)}) async-start(), calls=%async_computation.2 | async-start | bytes 2162688 | tf_op jit(solution)/shard_map/all_gather | solution.py:156
  13.4 12.5 %copy-start.16 = (f32[5,4096]{1,0:T(8,128)S(1)}, f32[5,4096]{1,0:T(8,128)}, u32[]{:S(2)}) copy-start(f32[5,4096]{1,0:T(8,128)} %param.26) | copy-start | bytes 245764
  13.4 13.3 %copy-start.19 = (bf16[256]{0:T(256)(128)(2,1)S(1)}, bf16[256]{0:T(256)(128)(2,1)}, u32[]{:S(2)}) copy-start(bf16[256]{0:T(256)(128)(2,1)} %param.24) | copy-start | bytes 1540
  13.4 53.6 %all-to-all-start = ((bf16[256,16,256]{2,0,1:T(8,128)(2,1)}), bf16[256,16,256]{2,0,1:T(8,128)(2,1)S(1)}, u32[]{:S(2)}, u32[]{:S(2)}) async-start(bf16[256,16,256]{2,0,1:T(8,128)(2,1)} %copy.154), calls=%async_computation | async-start | bytes 4194304 | tf_op jit(solution)/shard_map/all_to_all | solution.py:13
  22.9 205.3 %all-gather.10.cloned.1.call-start = ((), (), s32[]{:S(2)}) async-start(), calls=%async_computation.3 | async-start | bytes 2162688 | tf_op jit(solution)/shard_map/all_gather | solution.py:157
  23.7 297.1 %all-gather.18.cloned.1.call-start = ((), (), s32[]{:S(2)}) async-start(), calls=%async_computation.8 | async-start | bytes 4325376 | tf_op jit(solution)/shard_map/all_gather | solution.py:25
  24.6 2.2 collective-permute-start
  78.2 2.5 copy-start.3
  228.2 7.1 %copy-start.15 = (f32[4,64]{1,0:T(4,128)S(1)}, f32[4,64]{1,0:T(4,128)}, u32[]{:S(2)}) copy-start(f32[4,64]{1,0:T(4,128)} %param.34) | copy-start | bytes 3076
  235.4 15.5 %copy-start.20 = (s32[2]{0:T(128)S(1)}, s32[2]{0:T(128)}, u32[]{:S(2)}) copy-start(s32[2]{0:T(128)} %param.23) | copy-start | bytes 28
  235.4 16.2 %copy-start.11 = (f32[128,256]{0,1:T(8,128)S(1)}, f32[128,256]{0,1:T(8,128)}, u32[]{:S(2)}) copy-start(f32[128,256]{0,1:T(8,128)} %get-tuple-element.289) | copy-start | bytes 393220
  235.4 50.0 %copy-start.7 = (f32[128,256]{0,1:T(8,128)S(1)}, f32[128,256]{0,1:T(8,128)}, u32[]{:S(2)}) copy-start(f32[128,256]{0,1:T(8,128)} %get-tuple-element.290) | copy-start | bytes 393220
  248.9 0.7 copy-start.1
  248.9 36.6 %copy-start.10 = (f32[128,256]{0,1:T(8,128)S(1)}, f32[128,256]{0,1:T(8,128)}, u32[]{:S(2)}) copy-start(f32[128,256]{0,1:T(8,128)} %get-tuple-element.292) | copy-start | bytes 393220
  248.9 37.0 %copy-start.12 = (f32[128,256]{1,0:T(8,128)S(1)}, f32[128,256]{1,0:T(8,128)}, u32[]{:S(2)}) copy-start(f32[128,256]{1,0:T(8,128)} %get-tuple-element.296) | copy-start | bytes 393220
  249.6 141.7 %all-gather.14.cloned.1.call-start = ((), (), s32[]{:S(2)}) async-start(), calls=%async_computation.5 | async-start | bytes 2162688 | tf_op jit(solution)/shard_map/all_gather | solution.py:158
  250.2 213.6 %all-gather.16.cloned.1.call-start = ((), (), s32[]{:S(2)}) async-start(), calls=%async_computation.6 | async-start | bytes 2162688 | tf_op jit(solution)/shard_map/all_gather | solution.py:237
  250.8 310.9 %reduce-scatter.2.cloned.1.call-start = ((), (), s32[]{:S(2)}) async-start(), calls=%async_computation.7 | async-start | bytes 4456448 | tf_op jit(solution)/shard_map/reduce_scatter | solution.py:238
  250.9 34.4 %copy-start.17 = (f32[2,64]{1,0:T(2,128)}, f32[2,64]{1,0:T(2,128)S(1)}, u32[]{:S(2)}) copy-start(f32[2,64]{1,0:T(2,128)S(1)} %get-tuple-element.303) | copy-start | bytes 1540
  252.2 35.9 %copy-start.8 = (f32[2,64,4,64]{3,2,1,0:T(4,128)}, f32[2,64,4,64]{3,2,1,0:T(4,128)S(1)}, u32[]{:S(2)}) copy-start(f32[2,64,4,64]{3,2,1,0:T(4,128)S(1)} %fusion.67) | copy-start | bytes 393220
  288.1 2.4 copy-start.6
  288.1 2.6 copy-start.14
  374.5 89.4 %copy-start.4 = (bf16[256,16,256]{0,2,1:T(8,128)(2,1)S(1)}, bf16[256,16,256]{0,2,1:T(8,128)(2,1)}, u32[]{:S(2)}) copy-start(bf16[256,16,256]{0,2,1:T(8,128)(2,1)} %copy.155) | copy-start | bytes 6291460
  374.5 89.4 %copy-start.21 = (f32[256]{0:T(256)S(1)}, f32[256]{0:T(256)}, u32[]{:S(2)}) copy-start(f32[256]{0:T(256)} %param.36) | copy-start | bytes 3076
  374.5 89.3 %copy-start.22 = (f32[256]{0:T(256)S(1)}, f32[256]{0:T(256)}, u32[]{:S(2)}) copy-start(f32[256]{0:T(256)} %param.35) | copy-start | bytes 3076
  376.4 1.0 copy-start.5
  473.1 0.7 copy-start.18
  473.1 1.5 copy-start.9
  473.1 2.8 copy-start.2
  473.1 2.8 copy-start.13
Sparse Core Ops, SparseCore 0:
  10.1 76.1 all-gather.11
  88.5 68.8 all-gather.7
  159.5 68.6 all-gather.9
  249.7 71.0 all-gather.17
  322.8 68.4 all-gather.13
  393.2 70.5 all-gather.15
  473.2 88.4 reduce-scatter.1
